TPU v7x, 32 devices: a whole 2x2x4 slice. The times are simulated.
32 devices in a mesh: doc: 8 (over y, x, core), seq: 4 (over z).
Axes of the slice: x: 2, y: 2, z: 4, core: 2. Of those that a mesh axis runs over, the one named last changes fastest.
Arguments:
- inputs: bfloat16 [16, 1024, 768], P('doc', 'seq'), may hold values from -6 to 6
- attn_gain: float32 [768], replicated, may hold values from 0.5 to 1.5
- qkv_weight: bfloat16 [768, 2304], replicated, may hold values from -0.25 to 0.25
- attn_out_weight: bfloat16 [768, 768], replicated, may hold values from -2 to 2
- mlp_gain: float32 [768], replicated, may hold values from 0.5 to 1.5
- mlp_in_weight: bfloat16 [768, 2304], replicated, may hold values from -0.21875 to 0.21875
- mlp_out_weight: bfloat16 [1152, 768], replicated, may hold values from -0.1875 to 0.1875
- cotangent: bfloat16 [16, 1024, 768], P('doc', 'seq'), may hold values from -6 to 6
Outputs:
- output: bfloat16 [16, 1024, 768], P('doc', 'seq')
- input_grad: bfloat16 [16, 1024, 768], P('doc', 'seq')
- attn_gain_grad: float32 [768], replicated
- qkv_weight_grad: float32 [768, 2304], replicated
- attn_out_weight_grad: float32 [768, 768], replicated
- mlp_gain_grad: float32 [768], replicated
- mlp_in_weight_grad: float32 [768, 2304], replicated
- mlp_out_weight_grad: float32 [1152, 768], replicated
All inputs are finite; a program needn't handle non-finite values.
Results may differ from a plain program's by a relative error of at most 0.015.
Values may be sent and summed in bfloat16 or wider, within the bound.
A program may use at most 128 MiB of HBM per device.

v0:
```python
import jax
import jax.numpy as jnp
from jax import lax
from jax.sharding import PartitionSpec as P

HEAD_DIM = 64
ROPE_THETA = 160000.0
NORM_EPSILON = 1e-05


def norm_rows(values, scale_gain):
    row_mean = jnp.mean(values, axis=-1, keepdims=True)
    centered = values - row_mean
    variance = jnp.mean(centered * centered, axis=-1, keepdims=True)
    return centered * lax.rsqrt(variance + NORM_EPSILON) * scale_gain


def rotary_tables(positions, head_width):
    half_width = head_width // 2
    frequency = ROPE_THETA ** (-(jnp.arange(half_width, dtype=jnp.float32) * 2.0) / head_width)
    angles = positions.astype(jnp.float32)[:, None] * frequency[None, :]
    angles = jnp.concatenate([angles, angles], axis=-1)
    return (jnp.cos(angles)[:, None, :], jnp.sin(angles)[:, None, :])


def rotate(values, cosine_table, sine_table):
    half_width = values.shape[-1] // 2
    turned = jnp.concatenate([-values[..., half_width:], values[..., :half_width]], axis=-1)
    return values * cosine_table + turned * sine_table


def rotate_back(gradient, cosine_table, sine_table):
    half_width = gradient.shape[-1] // 2
    sined = gradient * sine_table
    turned = jnp.concatenate([sined[..., half_width:], -sined[..., :half_width]], axis=-1)
    return gradient * cosine_table + turned


def gelu_product(gate_up):
    half_width = gate_up.shape[-1] // 2
    return jax.nn.gelu(gate_up[..., :half_width], approximate=False) * gate_up[..., half_width:]


def split_heads(columns):
    return columns.reshape(columns.shape[0], columns.shape[1] // HEAD_DIM, HEAD_DIM)


def attend_forward(queries, key_rows, value_rows):
    length, features = queries.shape
    scores = (
        jnp.einsum(
            "qhd,khd->hqk",
            split_heads(queries),
            split_heads(key_rows),
            preferred_element_type=jnp.float32,
        )
        * 0.125
    )
    row_max = jnp.max(scores, axis=-1, keepdims=True)
    exp_scores = jnp.exp(scores - row_max)
    row_total = jnp.sum(exp_scores, axis=-1, keepdims=True)
    softmax_low = (exp_scores / row_total).astype(jnp.bfloat16)
    mixed_rows = jnp.einsum(
        "hqk,khd->qhd", softmax_low, split_heads(value_rows), preferred_element_type=jnp.float32
    )
    return (
        mixed_rows.reshape(length, features).astype(jnp.bfloat16),
        (row_max + jnp.log(row_total))[..., 0],
    )


def attend_backward(queries, key_rows, value_rows, grad_mixed, log_total, cosine_table, sine_table):
    length, features = queries.shape
    query_heads = split_heads(queries)
    key_heads = split_heads(key_rows)
    value_heads = split_heads(value_rows)
    grad_heads = split_heads(grad_mixed)
    scores = (
        jnp.einsum("qhd,khd->hqk", query_heads, key_heads, preferred_element_type=jnp.float32)
        * 0.125
    )
    softmax_out = jnp.exp(scores - log_total[..., None])
    grad_soft = jnp.einsum(
        "qhd,khd->hqk", grad_heads, value_heads, preferred_element_type=jnp.float32
    )
    row_inner = jnp.sum(softmax_out * grad_soft, axis=-1, keepdims=True)
    grad_scores = (softmax_out * (grad_soft - row_inner)).astype(jnp.bfloat16)
    grad_query = (
        jnp.einsum("hqk,khd->qhd", grad_scores, key_heads, preferred_element_type=jnp.float32)
        * 0.125
    )
    grad_key = (
        jnp.einsum("hqk,qhd->khd", grad_scores, query_heads, preferred_element_type=jnp.float32)
        * 0.125
    )
    grad_value = jnp.einsum(
        "hqk,qhd->khd",
        softmax_out.astype(jnp.bfloat16),
        grad_heads,
        preferred_element_type=jnp.float32,
    )
    grad_query = (
        rotate_back(grad_query, cosine_table, sine_table)
        .reshape(length, features)
        .astype(jnp.bfloat16)
    )
    grad_key = (
        rotate_back(grad_key, cosine_table, sine_table)
        .reshape(length, features)
        .astype(jnp.bfloat16)
    )
    return (grad_query, grad_key, grad_value.reshape(length, features).astype(jnp.bfloat16))


def per_device(
    inputs,
    attn_gain,
    qkv_weight,
    attn_out_weight,
    mlp_gain,
    mlp_in_weight,
    mlp_out_weight,
    cotangent,
):
    doc_count, row_count, features = inputs.shape
    token_count = doc_count * row_count
    length = row_count * lax.axis_size("seq")
    flat_in = inputs.reshape(token_count, features).astype(jnp.float32)
    normed = norm_rows(flat_in, attn_gain).astype(jnp.bfloat16)
    projected = jnp.dot(normed, qkv_weight, preferred_element_type=jnp.float32)
    projected = projected.reshape(doc_count, row_count, 3 * features)
    local_cos, local_sin = rotary_tables(
        lax.axis_index("seq") * row_count + jnp.arange(row_count, dtype=jnp.int32), HEAD_DIM
    )

    def turned_low(columns):
        shaped = columns.reshape(doc_count, row_count, features // HEAD_DIM, HEAD_DIM)
        return (
            rotate(shaped, local_cos, local_sin)
            .reshape(doc_count, row_count, features)
            .astype(jnp.bfloat16)
        )

    queries = turned_low(projected[..., :features])
    key_rows = turned_low(projected[..., features : 2 * features])
    value_rows = projected[..., 2 * features :].astype(jnp.bfloat16)
    head_queries, head_keys, head_values = (
        lax.all_to_all(queries, "seq", split_axis=2, concat_axis=1, tiled=True),
        lax.all_to_all(key_rows, "seq", split_axis=2, concat_axis=1, tiled=True),
        lax.all_to_all(value_rows, "seq", split_axis=2, concat_axis=1, tiled=True),
    )
    mixed_heads, log_total = lax.map(
        lambda bundle: attend_forward(*bundle), (head_queries, head_keys, head_values)
    )
    attended = lax.all_to_all(mixed_heads, "seq", split_axis=1, concat_axis=2, tiled=True).reshape(
        token_count, features
    )
    hidden_res = flat_in + jnp.dot(attended, attn_out_weight, preferred_element_type=jnp.float32)
    normed_two = norm_rows(hidden_res, mlp_gain).astype(jnp.bfloat16)
    gate_up = jnp.dot(normed_two, mlp_in_weight, preferred_element_type=jnp.float32)
    inner_act, inner_pull = jax.vjp(gelu_product, gate_up)
    inner_act = inner_act.astype(jnp.bfloat16)
    result = hidden_res + jnp.dot(inner_act, mlp_out_weight, preferred_element_type=jnp.float32)
    output = result.astype(jnp.bfloat16).reshape(doc_count, row_count, features)
    upstream = cotangent.reshape(token_count, features)
    grad_mlp_out = jnp.einsum("tf,td->fd", inner_act, upstream, preferred_element_type=jnp.float32)
    grad_inner = jnp.einsum(
        "td,fd->tf", upstream, mlp_out_weight, preferred_element_type=jnp.float32
    )
    grad_gate_up = inner_pull(grad_inner)[0].astype(jnp.bfloat16)
    grad_mlp_in = jnp.einsum(
        "td,tf->df", normed_two, grad_gate_up, preferred_element_type=jnp.float32
    )
    grad_normed_two = jnp.einsum(
        "tf,df->td", grad_gate_up, mlp_in_weight, preferred_element_type=jnp.float32
    )
    _, second_pull = jax.vjp(norm_rows, hidden_res, mlp_gain)
    grad_hidden, grad_mlp_gain = second_pull(grad_normed_two)
    grad_hidden = grad_hidden + upstream.astype(jnp.float32)
    grad_branch = grad_hidden.astype(jnp.bfloat16)
    grad_attn_out = jnp.einsum(
        "td,te->de", attended, grad_branch, preferred_element_type=jnp.float32
    )
    grad_attended = jnp.einsum(
        "te,de->td", grad_branch, attn_out_weight, preferred_element_type=jnp.float32
    )
    grad_attended = grad_attended.astype(jnp.bfloat16).reshape(doc_count, row_count, features)
    grad_mixed = lax.all_to_all(grad_attended, "seq", split_axis=2, concat_axis=1, tiled=True)
    full_cos, full_sin = rotary_tables(jnp.arange(length, dtype=jnp.int32), HEAD_DIM)
    grad_head_q, grad_head_k, grad_head_v = lax.map(
        lambda bundle: attend_backward(*bundle, full_cos, full_sin),
        (head_queries, head_keys, head_values, grad_mixed, log_total),
    )
    grad_tok_q, grad_tok_k, grad_tok_v = (
        lax.all_to_all(grad_head_q, "seq", split_axis=1, concat_axis=2, tiled=True),
        lax.all_to_all(grad_head_k, "seq", split_axis=1, concat_axis=2, tiled=True),
        lax.all_to_all(grad_head_v, "seq", split_axis=1, concat_axis=2, tiled=True),
    )
    grad_tok_q = grad_tok_q.reshape(token_count, features)
    grad_tok_k = grad_tok_k.reshape(token_count, features)
    grad_tok_v = grad_tok_v.reshape(token_count, features)
    grad_qkv = jnp.concatenate(
        [
            jnp.einsum("td,te->de", normed, grad_tok_q, preferred_element_type=jnp.float32),
            jnp.einsum("td,te->de", normed, grad_tok_k, preferred_element_type=jnp.float32),
            jnp.einsum("td,te->de", normed, grad_tok_v, preferred_element_type=jnp.float32),
        ],
        axis=1,
    )
    grad_normed = jnp.einsum(
        "te,de->td", grad_tok_q, qkv_weight[:, :features], preferred_element_type=jnp.float32
    )
    grad_normed = grad_normed + jnp.einsum(
        "te,de->td",
        grad_tok_k,
        qkv_weight[:, features : 2 * features],
        preferred_element_type=jnp.float32,
    )
    grad_normed = grad_normed + jnp.einsum(
        "te,de->td", grad_tok_v, qkv_weight[:, 2 * features :], preferred_element_type=jnp.float32
    )
    _, first_pull = jax.vjp(norm_rows, flat_in, attn_gain)
    grad_input, grad_attn_gain = first_pull(grad_normed)
    grad_input = (
        (grad_input + grad_hidden).astype(jnp.bfloat16).reshape(doc_count, row_count, features)
    )
    summed = lax.psum(
        (grad_attn_gain, grad_qkv, grad_attn_out, grad_mlp_gain, grad_mlp_in, grad_mlp_out),
        ("doc", "seq"),
    )
    return (output, grad_input, summed[0], summed[1], summed[2], summed[3], summed[4], summed[5])


def solution(mesh):
    placed = (P("doc", "seq", None), P(), P(), P(), P(), P(), P(), P("doc", "seq", None))
    return jax.shard_map(
        per_device,
        mesh=mesh,
        in_specs=placed,
        out_specs=(P("doc", "seq", None), P("doc", "seq", None), P(), P(), P(), P(), P(), P()),
        check_vma=False,
    )
```

profile of v0, /device:TPU:0, one launch (start us, length us, event | category | flops | bytes accessed | tf_op | source)
XLA Modules:
  0.0 743.3 jit_solution(14533819958164597936)
XLA Ops:
  12.8 4.3 fusion.13
  23.3 6.3 all-to-all-start
  29.6 3.9 fusion.58
  59.2 5.0 add_convert_fusion.3
  67.2 5.1 all-to-all-start.1
  75.3 16.6 %all-to-all-done.1 = bf16[2,256,768]{1,0,2:T(2,128)(2,1)} async-done(((bf16[2,256,768]{1,0,2:T(2,128)(2,1)}), bf16[2,256,768]{1,0,2:T(2,128)(2,1)}, u32[]{:S(2)}, u32[]{:S(2)}) %all-to-all-start.1) | async-done | bytes 786464 | tf_op jit(solution)/shard_map/all_to_all | solution.py:148
  91.9 4.4 all-to-all-start.2
  100.8 15.2 %all-to-all-done.2 = bf16[2,256,768]{1,0,2:T(2,128)(2,1)} async-done(((bf16[2,256,768]{1,0,2:T(2,128)(2,1)}), bf16[2,256,768]{1,0,2:T(2,128)(2,1)}, u32[]{:S(2)}, u32[]{:S(2)}) %all-to-all-start.2) | async-done | bytes 786464 | tf_op jit(solution)/shard_map/all_to_all | solution.py:149
  119.2 19.5 %while.26 = (s32[]{:T(128)}, bf16[2,1024,192]{1,2,0:T(8,128)(2,1)}, f32[2,3,1024]{2,1,0:T(4,128)}, bf16[2,1024,192]{1,2,0:T(8,128)(2,1)}, bf16[2,1024,192]{1,2,0...) while((s32[]{:T(128)}, bf16[2,1024,192]{1,2,0:T(8,128)(2,1)}, f32[2,3,1024]{2,1,0:T(4,128)}, ...), condition=%wide.region_5.6_spmd, body=%wide.region_2.5_spmd.sunk | while | flops 833811456 | bytes 48861340 | solution.py:152
  142.3 29.5 %all_to_all.132 = bf16[2,1024,192]{2,0,1:T(2,128)(2,1)} all-to-all(bf16[2,1024,192]{2,0,1:T(2,128)(2,1)} %copy.86), channel_id=1, replica_groups=mesh['doc'=8,'seq'=4] {'seq'}, dimensions={1} | all-to-all | bytes 1572864 | tf_op jit(solution)/shard_map/all_to_all | solution.py:155
  171.8 5.9 copy.87
  184.3 5.6 fusion.39
  205.8 17.4 %all-to-all-done.4 = bf16[2,256,768]{1,0,2:T(2,128)(2,1)S(1)} async-done(((bf16[2,256,768]{1,0,2:T(2,128)(2,1)}), bf16[2,256,768]{1,0,2:T(2,128)(2,1)S(1)}, u32[]{:S(2)}, u32[]{:S(2)}) %all-to-all-start.4) | async-done | bytes 786464 | tf_op jit(solution)/shard_map/all_to_all | solution.py:188
  227.2 60.3 %while.27 = (s32[]{:T(128)}, bf16[2,1024,192]{1,2,0:T(8,128)(2,1)}, bf16[2,1024,192]{1,2,0:T(8,128)(2,1)}, bf16[2,1024,192]{1,2,0:T(8,128)(2,1)}, bf16[2,1024,19...) while((s32[]{:T(128)}, bf16[2,1024,192]{1,2,0:T(8,128)(2,1)}, ...), condition=%wide.region_12.13_spmd, body=%wide.region_10.12_spmd.sunk | while | flops 2053501952 | bytes 154489168 | solution.py:190
  238.6 3.7 multiply_reduce_fusion.8
  242.3 5.3 multiply_convert_fusion.6
  247.6 4.1 convolution_bitcast_fusion.3
  268.8 3.7 multiply_reduce_fusion.8
  272.5 5.3 multiply_convert_fusion.6
  277.8 4.1 convolution_bitcast_fusion.3
  296.8 23.1 %all-to-all-done.7 = bf16[2,1024,192]{2,0,1:T(2,128)(2,1)S(1)} async-done(((bf16[2,1024,192]{2,0,1:T(2,128)(2,1)}), bf16[2,1024,192]{2,0,1:T(2,128)(2,1)S(1)}, u32[]{:S(2)}, u32[]{:S(2)}) %all-to-all-start.7) | async-done | bytes 786464 | tf_op jit(solution)/shard_map/all_to_all | solution.py:197
  325.5 23.1 %all-to-all-done.5 = bf16[2,1024,192]{2,0,1:T(2,128)(2,1)S(1)} async-done(((bf16[2,1024,192]{2,0,1:T(2,128)(2,1)}), bf16[2,1024,192]{2,0,1:T(2,128)(2,1)S(1)}, u32[]{:S(2)}, u32[]{:S(2)}) %all-to-all-start.5) | async-done | bytes 786464 | tf_op jit(solution)/shard_map/all_to_all | solution.py:195
  348.6 4.2 all-to-all-start.6
  360.9 5.2 fusion.40
  366.1 4.7 copy.96
  371.9 5.7 copy.92
  379.8 5.7 copy.94
  394.9 4.0 add_convert_fusion.2
  403.7 43.1 %all-reduce.2 = (f32[768]{0:T(1024)}, f32[768]{0:T(1024)}) all-reduce(f32[768]{0:T(1024)S(1)} %get-tuple-element.139, f32[768]{0:T(1024)S(1)} %copy-done.49), channel_id=1, replica_groups=mesh['doc'=8,'seq'=4] {'doc','seq'}, use_global_device_ids=true, to_apply=%region_16.17 | all-reduce | flops 1536 | bytes 12288 | tf_op jit(solution)/shard_map/psum | solution.py:227
  449.8 268.4 %all-reduce.6.cloned.1.call-done = (f32[768,2304]{0,1:T(8,128)}, f32[768,768]{1,0:T(8,128)}, f32[768,2304]{1,0:T(8,128)}, f32[1152,768]{1,0:T(8,128)}) async-done(((f32[768,2304]{0,1:T(8,128)}, f32[768,768]{1,0:T(8,128)}, f32[768,2304]{1,0:T(8,128)}, f32[1152,768]{1,0:T(8,128)}), (f32[768,2304]{0,1:T(8,128)}, f32[768,768]{1,0:T(8,128)}, f32[768,2304]{1,0:T(8,128)}, ...) | async-done | bytes 20054032 | tf_op jit(solution)/shard_map/psum | solution.py:227
  718.3 8.1 %copy.97 = f32[768,2304]{1,0:T(8,128)} copy(f32[768,2304]{0,1:T(8,128)} %get-tuple-element.177) | data formatting | bytes 14155776
  727.8 6.6 copy.145
  (252 shorter events, 180.5 us)
Async XLA Ops:
  7.2 174.9 %copy-start = (bf16[768,2304]{1,0:T(8,128)(2,1)S(1)}, bf16[768,2304]{1,0:T(8,128)(2,1)}, u32[]{:S(2)}) copy-start(bf16[768,2304]{1,0:T(8,128)(2,1)} %param.17) | copy-start | bytes 10616836
  12.8 4.3 copy-start.8
  23.3 43.9 %all-to-all-start = ((bf16[2,256,768]{1,0,2:T(2,128)(2,1)}), bf16[2,256,768]{1,0,2:T(2,128)(2,1)}, u32[]{:S(2)}, u32[]{:S(2)}) async-start(bf16[2,256,768]{1,0,2:T(2,128)(2,1)} %copy.71), calls=%async_computation | async-start | bytes 1572864 | tf_op jit(solution)/shard_map/all_to_all | solution.py:150
  33.5 8.8 %copy-start.50 = (f32[32]{0:T(128)}, f32[32]{0:T(128)S(1)}, u32[]{:S(2)}) copy-start(f32[32]{0:T(128)S(1)} %multiply_power_fusion) | copy-start | bytes 388
  67.2 24.7 %all-to-all-start.1 = ((bf16[2,256,768]{1,0,2:T(2,128)(2,1)}), bf16[2,256,768]{1,0,2:T(2,128)(2,1)}, u32[]{:S(2)}, u32[]{:S(2)}) async-start(bf16[2,256,768]{1,0,2:T(2,128)(2,1)} %copy.78), calls=%async_computation.1 | async-start | bytes 1572864 | tf_op jit(solution)/shard_map/all_to_all | solution.py:148
  91.9 24.0 %all-to-all-start.2 = ((bf16[2,256,768]{1,0,2:T(2,128)(2,1)}), bf16[2,256,768]{1,0,2:T(2,128)(2,1)}, u32[]{:S(2)}, u32[]{:S(2)}) async-start(bf16[2,256,768]{1,0,2:T(2,128)(2,1)} %copy.83), calls=%async_computation.2 | async-start | bytes 1572864 | tf_op jit(solution)/shard_map/all_to_all | solution.py:149
  181.7 13.2 %copy-start.6 = (f32[512,768]{1,0:T(8,128)}, f32[512,768]{1,0:T(8,128)S(1)}, u32[]{:S(2)}) copy-start(f32[512,768]{1,0:T(8,128)S(1)} %get-tuple-element.225) | copy-start | bytes 4718596
  181.8 13.2 %copy-start.41 = (f32[512]{0:T(512)}, f32[512]{0:T(512)S(1)}, u32[]{:S(2)}) copy-start(f32[512]{0:T(512)S(1)} %broadcast_multiply_fusion.3) | copy-start | bytes 6148
  182.1 12.8 %copy-start.43 = (f32[512]{0:T(512)}, f32[512]{0:T(512)S(1)}, u32[]{:S(2)}) copy-start(f32[512]{0:T(512)S(1)} %fusion.46) | copy-start | bytes 6148
  198.7 5.3 copy-start.51
  200.5 22.6 %all-to-all-start.4 = ((bf16[2,256,768]{1,0,2:T(2,128)(2,1)}), bf16[2,256,768]{1,0,2:T(2,128)(2,1)S(1)}, u32[]{:S(2)}, u32[]{:S(2)}) async-start(bf16[2,256,768]{1,0,2:T(2,128)(2,1)} %copy.88), calls=%async_computation.4 | async-start | bytes 1572864 | tf_op jit(solution)/shard_map/all_to_all | solution.py:188
  247.6 4.6 copy-start.2
  277.8 4.6 copy-start.2
  287.5 7.2 copy-start.22
  291.2 28.7 %all-to-all-start.7 = ((bf16[2,1024,192]{2,0,1:T(2,128)(2,1)}), bf16[2,1024,192]{2,0,1:T(2,128)(2,1)S(1)}, u32[]{:S(2)}, u32[]{:S(2)}) async-start(bf16[2,1024,192]{2,0,1:T(2,128)(2,1)} %copy.95), calls=%async_computation.7 | async-start | bytes 2097152 | tf_op jit(solution)/shard_map/all_to_all | solution.py:197
  294.7 28.7 %copy-start.25 = (bf16[2,1024,192]{1,2,0:T(8,128)(2,1)S(1)}, bf16[2,1024,192]{1,2,0:T(8,128)(2,1)}, u32[]{:S(2)}) copy-start(bf16[2,1024,192]{1,2,0:T(8,128)(2,1)} %get-tuple-element.103) | copy-start | bytes 2359300
  319.9 28.7 %copy-start.17 = (bf16[2,1024,192]{2,0,1:T(2,128)(2,1)}, bf16[2,1024,192]{2,0,1:T(2,128)(2,1)S(1)}, u32[]{:S(2)}) copy-start(bf16[2,1024,192]{2,0,1:T(2,128)(2,1)S(1)} %all-to-all-done.7) | copy-start | bytes 2359300
  319.9 28.7 %all-to-all-start.5 = ((bf16[2,1024,192]{2,0,1:T(2,128)(2,1)}), bf16[2,1024,192]{2,0,1:T(2,128)(2,1)S(1)}, u32[]{:S(2)}, u32[]{:S(2)}) async-start(bf16[2,1024,192]{2,0,1:T(2,128)(2,1)} %copy.91), calls=%async_computation.5 | async-start | bytes 2097152 | tf_op jit(solution)/shard_map/all_to_all | solution.py:195
  348.6 8.1 %copy-start.18 = (bf16[2,1024,192]{2,0,1:T(2,128)(2,1)}, bf16[2,1024,192]{2,0,1:T(2,128)(2,1)S(1)}, u32[]{:S(2)}) copy-start(bf16[2,1024,192]{2,0,1:T(2,128)(2,1)S(1)} %all-to-all-done.5) | copy-start | bytes 2359300
  348.6 31.2 %all-to-all-start.6 = ((bf16[2,1024,192]{2,0,1:T(2,128)(2,1)}), bf16[2,1024,192]{2,0,1:T(2,128)(2,1)}, u32[]{:S(2)}, u32[]{:S(2)}) async-start(bf16[2,1024,192]{2,0,1:T(2,128)(2,1)} %copy.93), calls=%async_computation.6 | async-start | bytes 2097152 | tf_op jit(solution)/shard_map/all_to_all | solution.py:196
  352.9 365.4 %all-reduce.6.cloned.1.call-start = ((), (), s32[]{:S(2)}) async-start(), calls=%async_computation.8 | async-start | bytes 40108032 | tf_op jit(solution)/shard_map/psum | solution.py:227
  356.8 4.1 copy-start.36
  356.8 4.1 copy-start.39
  356.8 4.1 copy-start.42
  356.8 4.1 copy-start.44
  377.6 9.3 %copy-start.9 = (bf16[2,256,768]{2,1,0:T(8,128)(2,1)S(1)}, bf16[2,256,768]{2,1,0:T(8,128)(2,1)}, u32[]{:S(2)}) copy-start(bf16[2,256,768]{2,1,0:T(8,128)(2,1)} %copy-done.8) | copy-start | bytes 2359300
  394.9 4.1 copy-start.30
  394.9 4.1 copy-start.37
  402.9 44.0 %copy-start.46 = (f32[512]{0:T(512)S(1)}, f32[512]{0:T(512)}, u32[]{:S(2)}) copy-start(f32[512]{0:T(512)} %copy-done.45) | copy-start | bytes 6148
  718.3 8.1 %copy-start.34 = (f32[768,768]{1,0:T(8,128)S(1)}, f32[768,768]{1,0:T(8,128)}, u32[]{:S(2)}) copy-start(f32[768,768]{1,0:T(8,128)} %get-tuple-element.433) | copy-start | bytes 7077892
  727.8 6.6 copy-start.19
  727.8 8.4 %copy-start.1 = (bf16[768,2304]{1,0:T(8,128)(2,1)S(1)}, bf16[768,2304]{1,0:T(8,128)(2,1)}, u32[]{:S(2)}) copy-start(bf16[768,2304]{1,0:T(8,128)(2,1)} %param.17) | copy-start | bytes 10616836
  (38 other events, 68.1 us)
Sparse Core Ops, SparseCore 0:
  394.3 323.9 all-reduce.5
where the time goes:
time: 752 us; the launch traced here: 743 us
  waiting for transfers between devices  364 us (48%)
  local copies, waits for them, and re-layouts  133 us (18%)
  matrix products  77.8 us (10%)
  blocking collectives  72.7 us (10%)
  other arithmetic  49.8 us (7%)
  starting transfers between devices  30.8 us (4%)
  between operations  14.9 us (2%)
    psum x1, waiting for transfers between devices, per_device(): lax.psum((grad_attn_gain, grad_qkv, grad_attn_out, grad_mlp_gain, grad_ml...  268 us
    psum x1, blocking collectives, per_device(): lax.psum((grad_attn_gain, grad_qkv, grad_attn_out, grad_mlp_gain, grad_ml...  43.1 us
    unnamed x102, local copies, waits for them, and re-layouts  30.9 us
    all_to_all x1, blocking collectives, per_device(): lax.all_to_all(mixed_heads, 'seq', split_axis=1, concat_axis=2, tiled=True)  29.5 us
    all_to_all x1, waiting for transfers between devices, per_device(): lax.all_to_all(grad_head_v, 'seq', split_axis=1, concat_axis=2, tiled=True)  23.1 us
    all_to_all x1, waiting for transfers between devices, per_device(): lax.all_to_all(grad_head_q, 'seq', split_axis=1, concat_axis=2, tiled=True)  23.1 us
    all_to_all x1, waiting for transfers between devices, per_device(): lax.all_to_all(grad_attended, 'seq', split_axis=2, concat_axis=1, tiled=T...  17.4 us
    all_to_all x1, waiting for transfers between devices, per_device(): lax.all_to_all(queries, 'seq', split_axis=2, concat_axis=1, tiled=True)  16.6 us
  transfers between devices with their start and end apart: 8, of which 6 were waited for; matrix products, arithmetic and copies ran while one was open for 12% of the time, Pallas kernels for 0%

commit v1 on v0

--- a/solution.py
+++ b/solution.py
@@ -6,6 +6,11 @@
 HEAD_DIM = 64
 ROPE_THETA = 160000.0
 NORM_EPSILON = 1e-05
+
+
+def axis_by_axis(value, first, second):
+    half = lax.psum(value, first)
+    return lax.psum(half, second)
 
 
 def norm_rows(values, scale_gain):
@@ -224,9 +229,10 @@
     grad_input = (
         (grad_input + grad_hidden).astype(jnp.bfloat16).reshape(doc_count, row_count, features)
     )
-    summed = lax.psum(
+    summed = axis_by_axis(
         (grad_attn_gain, grad_qkv, grad_attn_out, grad_mlp_gain, grad_mlp_in, grad_mlp_out),
-        ("doc", "seq"),
+        "seq",
+        "doc",
     )
     return (output, grad_input, summed[0], summed[1], summed[2], summed[3], summed[4], summed[5])
 

time: 752 us -> 1360 us (1.81)
  waiting for transfers between devices: 364 us -> 989 us
  blocking collectives: 72.7 us -> 53.3 us
    psum x1 -> x2, waiting for transfers between devices: 268 us -> 894 us  [the longest x1 672 us: axis_by_axis(): half = lax.psum(value, first)]
    psum x1 -> x2, blocking collectives: 43.1 us -> 23.8 us  [the longest x1 14.3 us: axis_by_axis(): return lax.psum(half, second)]
  transfers between devices with their start and end apart: 8 -> 9, of which waited for: 6 -> 7; matrix products, arithmetic and copies ran while one was open for 12% -> 6% of each run, Pallas kernels for 0% -> 0%
where the time goes in v1:
time: 1360 us; the launch traced here: 1350 us
  waiting for transfers between devices  989 us (73%)
  local copies, waits for them, and re-layouts  133 us (10%)
  matrix products  77.8 us (6%)
  blocking collectives  53.3 us (4%)
  other arithmetic  49.9 us (4%)
  starting transfers between devices  30.8 us (2%)
  between operations  14.9 us (1%)
    psum x1, waiting for transfers between devices, axis_by_axis(): half = lax.psum(value, first)  672 us
    psum x1, waiting for transfers between devices, axis_by_axis(): return lax.psum(half, second)  222 us
    unnamed x102, local copies, waits for them, and re-layouts  30.7 us
    all_to_all x1, blocking collectives, per_device(): lax.all_to_all(mixed_heads, 'seq', split_axis=1, concat_axis=2, tiled=True)  29.5 us
  transfers between devices with their start and end apart: 9, of which 7 were waited for; matrix products, arithmetic and copies ran while one was open for 6% of the time, Pallas kernels for 0%

profile of v1, /device:TPU:0, one launch (start us, length us, event | category | flops | bytes accessed | tf_op | source)
XLA Modules:
  0.0 1348.9 jit_solution(8615729528079659737)
XLA Ops:
  12.8 4.3 fusion.13
  23.3 6.3 all-to-all-start
  29.6 3.9 fusion.58
  59.2 5.0 add_convert_fusion.3
  67.2 5.1 all-to-all-start.1
  75.3 16.6 %all-to-all-done.1 = bf16[2,256,768]{1,0,2:T(2,128)(2,1)} async-done(((bf16[2,256,768]{1,0,2:T(2,128)(2,1)}), bf16[2,256,768]{1,0,2:T(2,128)(2,1)}, u32[]{:S(2)}, u32[]{:S(2)}) %all-to-all-start.1) | async-done | bytes 786464 | tf_op jit(solution)/shard_map/all_to_all | solution.py:153
  91.9 4.4 all-to-all-start.2
  100.7 15.2 %all-to-all-done.2 = bf16[2,256,768]{1,0,2:T(2,128)(2,1)} async-done(((bf16[2,256,768]{1,0,2:T(2,128)(2,1)}), bf16[2,256,768]{1,0,2:T(2,128)(2,1)}, u32[]{:S(2)}, u32[]{:S(2)}) %all-to-all-start.2) | async-done | bytes 786464 | tf_op jit(solution)/shard_map/all_to_all | solution.py:154
  119.2 19.5 %while.26 = (s32[]{:T(128)}, bf16[2,1024,192]{1,2,0:T(8,128)(2,1)}, f32[2,3,1024]{2,1,0:T(4,128)}, bf16[2,1024,192]{1,2,0:T(8,128)(2,1)}, bf16[2,1024,192]{1,2,0...) while((s32[]{:T(128)}, bf16[2,1024,192]{1,2,0:T(8,128)(2,1)}, f32[2,3,1024]{2,1,0:T(4,128)}, ...), condition=%wide.region_5.6_spmd, body=%wide.region_2.5_spmd.sunk | while | flops 833811456 | bytes 48861340 | solution.py:157
  142.3 29.5 %all_to_all.132 = bf16[2,1024,192]{2,0,1:T(2,128)(2,1)} all-to-all(bf16[2,1024,192]{2,0,1:T(2,128)(2,1)} %copy.86), channel_id=1, replica_groups=mesh['doc'=8,'seq'=4] {'seq'}, dimensions={1} | all-to-all | bytes 1572864 | tf_op jit(solution)/shard_map/all_to_all | solution.py:160
  171.8 5.9 copy.87
  184.3 5.6 fusion.39
  205.8 17.4 %all-to-all-done.4 = bf16[2,256,768]{1,0,2:T(2,128)(2,1)S(1)} async-done(((bf16[2,256,768]{1,0,2:T(2,128)(2,1)}), bf16[2,256,768]{1,0,2:T(2,128)(2,1)S(1)}, u32[]{:S(2)}, u32[]{:S(2)}) %all-to-all-start.4) | async-done | bytes 786464 | tf_op jit(solution)/shard_map/all_to_all | solution.py:193
  227.3 60.3 %while.27 = (s32[]{:T(128)}, bf16[2,1024,192]{1,2,0:T(8,128)(2,1)}, bf16[2,1024,192]{1,2,0:T(8,128)(2,1)}, bf16[2,1024,192]{1,2,0:T(8,128)(2,1)}, bf16[2,1024,19...) while((s32[]{:T(128)}, bf16[2,1024,192]{1,2,0:T(8,128)(2,1)}, ...), condition=%wide.region_12.13_spmd, body=%wide.region_10.12_spmd.sunk | while | flops 2053501952 | bytes 154489168 | solution.py:195
  242.4 5.3 multiply_convert_fusion.6
  247.7 4.1 convolution_bitcast_fusion.3
  272.6 5.3 multiply_convert_fusion.6
  277.9 4.1 convolution_bitcast_fusion.3
  296.8 23.1 %all-to-all-done.7 = bf16[2,1024,192]{2,0,1:T(2,128)(2,1)S(1)} async-done(((bf16[2,1024,192]{2,0,1:T(2,128)(2,1)}), bf16[2,1024,192]{2,0,1:T(2,128)(2,1)S(1)}, u32[]{:S(2)}, u32[]{:S(2)}) %all-to-all-start.7) | async-done | bytes 786464 | tf_op jit(solution)/shard_map/all_to_all | solution.py:202
  325.6 23.1 %all-to-all-done.5 = bf16[2,1024,192]{2,0,1:T(2,128)(2,1)S(1)} async-done(((bf16[2,1024,192]{2,0,1:T(2,128)(2,1)}), bf16[2,1024,192]{2,0,1:T(2,128)(2,1)S(1)}, u32[]{:S(2)}, u32[]{:S(2)}) %all-to-all-start.5) | async-done | bytes 786464 | tf_op jit(solution)/shard_map/all_to_all | solution.py:200
  348.7 4.2 all-to-all-start.6
  361.0 5.2 fusion.40
  366.2 4.7 copy.96
  372.0 5.7 copy.92
  379.9 5.7 copy.94
  394.3 672.0 %all-reduce.11.cloned.1.call-done = (f32[768,2304]{0,1:T(8,128)}, f32[768,768]{1,0:T(8,128)}, f32[768,2304]{1,0:T(8,128)}, f32[1152,768]{1,0:T(8,128)}) async-done(((f32[768,2304]{0,1:T(8,128)}, f32[768,768]{1,0:T(8,128)}, f32[768,2304]{1,0:T(8,128)}, f32[1152,768]{1,0:T(8,128)}), (f32[768,2304]{0,1:T(8,128)}, f32[768,768]{1,0:T(8,128)}, f32[768,2304]{1,0:T(8,128)}, ...) | async-done | bytes 20054032 | tf_op jit(solution)/shard_map/psum | solution.py:12
  1067.0 4.1 add_convert_fusion.2
  1075.6 9.5 all-reduce.4
  1085.1 14.3 %all-reduce.2 = (f32[768]{0:T(1024)}, f32[768]{0:T(1024)}) all-reduce(f32[768]{0:T(1024)S(1)} %get-tuple-element.181, f32[768]{0:T(1024)S(1)} %get-tuple-element.182), channel_id=1, replica_groups=mesh['doc'=8,'seq'=4] {'doc'}, use_global_device_ids=true, to_apply=%region_17.18 | all-reduce | flops 1536 | bytes 12288 | tf_op jit(solution)/shard_map/psum | solution.py:13
  1102.4 221.5 %all-reduce.9.cloned.1.call-done = (f32[768,2304]{0,1:T(8,128)}, f32[768,768]{1,0:T(8,128)}, f32[768,2304]{1,0:T(8,128)}, f32[1152,768]{1,0:T(8,128)}) async-done(((f32[768,2304]{0,1:T(8,128)}, f32[768,768]{1,0:T(8,128)}, f32[768,2304]{1,0:T(8,128)}, f32[1152,768]{1,0:T(8,128)}), (f32[768,2304]{0,1:T(8,128)}, f32[768,768]{1,0:T(8,128)}, f32[768,2304]{1,0:T(8,128)}, ...) | async-done | bytes 20054032 | tf_op jit(solution)/shard_map/psum | solution.py:13
  1324.0 8.1 copy.97
  1333.5 6.6 copy.149
  (256 shorter events, 188.0 us)
Async XLA Ops:
  7.2 174.9 %copy-start = (bf16[768,2304]{1,0:T(8,128)(2,1)S(1)}, bf16[768,2304]{1,0:T(8,128)(2,1)}, u32[]{:S(2)}) copy-start(bf16[768,2304]{1,0:T(8,128)(2,1)} %param.17) | copy-start | bytes 10616836
  12.8 4.3 copy-start.8
  23.3 43.9 %all-to-all-start = ((bf16[2,256,768]{1,0,2:T(2,128)(2,1)}), bf16[2,256,768]{1,0,2:T(2,128)(2,1)}, u32[]{:S(2)}, u32[]{:S(2)}) async-start(bf16[2,256,768]{1,0,2:T(2,128)(2,1)} %copy.71), calls=%async_computation | async-start | bytes 1572864 | tf_op jit(solution)/shard_map/all_to_all | solution.py:155
  33.4 8.8 copy-start.50
  67.2 24.7 %all-to-all-start.1 = ((bf16[2,256,768]{1,0,2:T(2,128)(2,1)}), bf16[2,256,768]{1,0,2:T(2,128)(2,1)}, u32[]{:S(2)}, u32[]{:S(2)}) async-start(bf16[2,256,768]{1,0,2:T(2,128)(2,1)} %copy.78), calls=%async_computation.1 | async-start | bytes 1572864 | tf_op jit(solution)/shard_map/all_to_all | solution.py:153
  91.9 24.0 %all-to-all-start.2 = ((bf16[2,256,768]{1,0,2:T(2,128)(2,1)}), bf16[2,256,768]{1,0,2:T(2,128)(2,1)}, u32[]{:S(2)}, u32[]{:S(2)}) async-start(bf16[2,256,768]{1,0,2:T(2,128)(2,1)} %copy.83), calls=%async_computation.2 | async-start | bytes 1572864 | tf_op jit(solution)/shard_map/all_to_all | solution.py:154
  181.7 13.2 copy-start.6
  181.8 13.2 copy-start.41
  182.1 12.9 copy-start.43
  198.8 5.3 copy-start.51
  200.6 22.6 %all-to-all-start.4 = ((bf16[2,256,768]{1,0,2:T(2,128)(2,1)}), bf16[2,256,768]{1,0,2:T(2,128)(2,1)S(1)}, u32[]{:S(2)}, u32[]{:S(2)}) async-start(bf16[2,256,768]{1,0,2:T(2,128)(2,1)} %copy.88), calls=%async_computation.4 | async-start | bytes 1572864 | tf_op jit(solution)/shard_map/all_to_all | solution.py:193
  247.7 4.6 copy-start.2
  277.9 4.6 copy-start.2
  287.6 7.2 copy-start.22
  291.3 28.7 %all-to-all-start.7 = ((bf16[2,1024,192]{2,0,1:T(2,128)(2,1)}), bf16[2,1024,192]{2,0,1:T(2,128)(2,1)S(1)}, u32[]{:S(2)}, u32[]{:S(2)}) async-start(bf16[2,1024,192]{2,0,1:T(2,128)(2,1)} %copy.95), calls=%async_computation.7 | async-start | bytes 2097152 | tf_op jit(solution)/shard_map/all_to_all | solution.py:202
  294.8 28.7 %copy-start.25 = (bf16[2,1024,192]{1,2,0:T(8,128)(2,1)S(1)}, bf16[2,1024,192]{1,2,0:T(8,128)(2,1)}, u32[]{:S(2)}) copy-start(bf16[2,1024,192]{1,2,0:T(8,128)(2,1)} %get-tuple-element.103) | copy-start | bytes 2359300
  320.0 28.7 %copy-start.17 = (bf16[2,1024,192]{2,0,1:T(2,128)(2,1)}, bf16[2,1024,192]{2,0,1:T(2,128)(2,1)S(1)}, u32[]{:S(2)}) copy-start(bf16[2,1024,192]{2,0,1:T(2,128)(2,1)S(1)} %all-to-all-done.7) | copy-start | bytes 2359300
  320.0 28.7 %all-to-all-start.5 = ((bf16[2,1024,192]{2,0,1:T(2,128)(2,1)}), bf16[2,1024,192]{2,0,1:T(2,128)(2,1)S(1)}, u32[]{:S(2)}, u32[]{:S(2)}) async-start(bf16[2,1024,192]{2,0,1:T(2,128)(2,1)} %copy.91), calls=%async_computation.5 | async-start | bytes 2097152 | tf_op jit(solution)/shard_map/all_to_all | solution.py:200
  348.7 8.1 copy-start.18
  348.7 31.2 %all-to-all-start.6 = ((bf16[2,1024,192]{2,0,1:T(2,128)(2,1)}), bf16[2,1024,192]{2,0,1:T(2,128)(2,1)}, u32[]{:S(2)}, u32[]{:S(2)}) async-start(bf16[2,1024,192]{2,0,1:T(2,128)(2,1)} %copy.93), calls=%async_computation.6 | async-start | bytes 2097152 | tf_op jit(solution)/shard_map/all_to_all | solution.py:201
  353.0 713.4 %all-reduce.11.cloned.1.call-start = ((), (), s32[]{:S(2)}) async-start(), calls=%async_computation.9 | async-start | bytes 40108032 | tf_op jit(solution)/shard_map/psum | solution.py:12
  356.9 4.1 copy-start.36
  356.9 4.1 copy-start.39
  356.9 4.1 copy-start.42
  356.9 4.1 copy-start.44
  377.7 9.3 copy-start.9
  394.3 929.7 %all-reduce.9.cloned.1.call-start = ((), (), s32[]{:S(2)}) async-start(), calls=%async_computation.8 | async-start | bytes 40108032 | tf_op jit(solution)/shard_map/psum | solution.py:13
  1067.0 4.1 copy-start.30
  1074.8 24.6 %copy-start.46 = (f32[512]{0:T(512)S(1)}, f32[512]{0:T(512)}, u32[]{:S(2)}) copy-start(f32[512]{0:T(512)} %copy-done.45) | copy-start | bytes 6148
  1324.0 8.1 copy-start.34
  1333.5 6.6 copy-start.19
  1333.5 8.4 copy-start.1
  (39 other events, 71.7 us)
Sparse Core Ops, SparseCore 0:
  394.4 671.8 all-reduce.10
  1070.6 253.2 all-reduce.8
